TPU v7x, 512 devices: a whole 4x4x16 slice. The times are simulated.
512 devices in a mesh: dp: 64 (over z, x_hi, core), mp: 8 (over x_lo, y).
Axes of the slice: x: 4 (x_hi: 2, x_lo: 2; x = x_hi * 2 + x_lo), y: 4, z: 16, core: 2. Of those that a mesh axis runs over, the one named last changes fastest.
Arguments:
- normed_input_rows: bfloat16 [24576, 8192], P('dp', 'mp'), may hold values from -6 to 6
- frozen_queries: bfloat16 [24576, 8192], P('dp', 'mp'), may hold values from -6 to 6
- frozen_keys: bfloat16 [24576, 1024], P('dp', 'mp'), may hold values from -6 to 6
- frozen_values: bfloat16 [24576, 1024], P('dp', 'mp'), may hold values from -6 to 6
- attention_output_gradient: bfloat16 [24576, 8192], P('dp', 'mp'), may hold values from -1.1953125 to 1.1953125
- adapter_down_weight: float32 [64, 8192, 192], P(None, ('mp', 'dp')), may hold values from -0.0625 to 0.0625
- adapter_up_query: float32 [64, 64, 8192], P(None, 'dp', 'mp'), may hold values from -0.75 to 0.75
- adapter_up_key_value: float32 [64, 64, 8, 256], P(None, 'dp', 'mp'), may hold values from -0.75 to 0.75
- document_numbers: int32 [24576], P('dp'), may hold values from 0 to 1535, as said below
- block_tenant_slot: int32 [192], P('dp'), may hold values from 0 to 1, as said below
- shard_tenant_table: int32 [64, 2], replicated, may hold values from 0 to 63, as said below
Outputs:
- grad_down: float32 [64, 8192, 192], P(None, ('mp', 'dp'))
- grad_upq: float32 [64, 64, 8192], P(None, 'dp', 'mp')
- grad_upkv: float32 [64, 64, 8, 256], P(None, 'dp', 'mp')
Inputs may be any that keep to these rules, and one draw needn't show every extreme that they name: `document_numbers`: document numbers never fall along the rows; a document starts only at a multiple of 16 rows, always at the first row of each index of dp, at the last 16 rows of all, and wherever the slot of a block changes; a document's number is its first row divided by 16. `block_tenant_slot`: the 3 blocks of each index of dp name slots in an order that never falls, and every one of the 2 slots is named. `shard_tenant_table`: each row holds 2 distinct tenants.
All inputs are finite; a program needn't handle non-finite values.
Results may differ from a plain program's by a relative error of at most 0.012.
The roundings to bfloat16 on the way count: a program that leaves them out, or rounds other values in their place, can miss the bound.
Values sent between devices are 32-bit elements; how exact they have to be, the bound alone decides.
A program may use at most 64 MiB of HBM per device.

v0:
```python
import jax
import jax.numpy as jnp
from jax import lax
from jax.sharding import PartitionSpec as P

ADAPTER_SCALE = 0.5
MASKED = -1e30
PRECISION_HIGH = lax.Precision.HIGHEST


def attention_grads(query_row_block, key_row_block, value_row_block, upstream, doc_row):
    row_total = query_row_block.shape[0]
    kv_heads = key_row_block.shape[1]
    groups = query_row_block.shape[1] // kv_heads
    head_size = query_row_block.shape[2]
    query_g = query_row_block.reshape(row_total, kv_heads, groups, head_size)
    upstream_g = upstream.reshape(row_total, kv_heads, groups, head_size)
    inverse = 1.0 / head_size**0.5
    scores = (
        jnp.einsum("qkgd,jkd->kgqj", query_g, key_row_block, preferred_element_type=jnp.float32)
        * inverse
    )
    position = jnp.arange(row_total, dtype=jnp.int32)
    allowed = (doc_row[:, None] == doc_row[None, :]) & (position[:, None] >= position[None, :])
    scores = jnp.where(allowed, scores, MASKED)
    row_top = jnp.max(scores, axis=-1, keepdims=True)
    weights = jnp.exp(scores - row_top)
    attn_probs = weights / jnp.sum(weights, axis=-1, keepdims=True)
    probs_low = attn_probs.astype(jnp.bfloat16)
    grad_probs = jnp.einsum(
        "qkgd,jkd->kgqj", upstream_g, value_row_block, preferred_element_type=jnp.float32
    )
    row_inner = jnp.sum(attn_probs * grad_probs, axis=-1, keepdims=True)
    grad_scores = (attn_probs * (grad_probs - row_inner) * inverse).astype(jnp.bfloat16)
    grad_query = jnp.einsum(
        "kgqj,jkd->qkgd", grad_scores, key_row_block, preferred_element_type=jnp.float32
    ).reshape(row_total, -1)
    key_gradient = jnp.einsum(
        "kgqj,qkgd->jkd", grad_scores, query_g, preferred_element_type=jnp.float32
    ).reshape(row_total, -1)
    value_gradient = jnp.einsum(
        "kgqj,qkgd->jkd", probs_low, upstream_g, preferred_element_type=jnp.float32
    ).reshape(row_total, -1)
    return (grad_query, key_gradient, value_gradient)


def adapted(frozen_rows, low_part, panel_cols):
    extra_term = jnp.einsum("brk,bkc->brc", low_part, panel_cols, precision=PRECISION_HIGH)
    extra_term = extra_term.reshape(frozen_rows.shape[0], -1)
    return (frozen_rows.astype(jnp.float32) + ADAPTER_SCALE * extra_term).astype(jnp.bfloat16)


def on_device(
    normed_input_rows,
    frozen_queries,
    frozen_keys,
    frozen_values,
    attention_output_gradient,
    adapter_down_weight,
    adapter_up_query,
    adapter_up_key_value,
    document_numbers,
    block_tenant_slot,
    shard_tenant_table,
):
    row_count = normed_input_rows.shape[0]
    block_count = block_tenant_slot.shape[0]
    block_rows = row_count // block_count
    dp_count = lax.axis_size("dp")
    count_of_tenants = adapter_down_weight.shape[0]
    desired_result = shard_tenant_table.reshape(-1)
    down_panels, upq_panels, upkv_panels = (
        lax.all_to_all(
            adapter_down_weight[desired_result], "dp", split_axis=0, concat_axis=1, tiled=True
        ),
        lax.all_to_all(
            adapter_up_query[desired_result], "dp", split_axis=0, concat_axis=1, tiled=True
        ),
        lax.all_to_all(
            adapter_up_key_value[desired_result], "dp", split_axis=0, concat_axis=1, tiled=True
        ),
    )
    adapter_rank = down_panels.shape[2] // 3
    row_blocks = normed_input_rows.reshape(block_count, block_rows, -1).astype(jnp.float32)
    partial_down = jnp.einsum(
        "bri,bij->brj", row_blocks, down_panels[block_tenant_slot], precision=PRECISION_HIGH
    )
    lowrank = lax.psum(partial_down.reshape(row_count, 3 * adapter_rank), "mp")
    head_size = upkv_panels.shape[3] // 2
    kv_heads = upkv_panels.shape[2]
    query_heads = frozen_queries.shape[1] // head_size
    low_blocks = lowrank.reshape(block_count, block_rows, 3, adapter_rank)
    upq_blocks = upq_panels[block_tenant_slot]
    upkv_blocks = upkv_panels[block_tenant_slot]
    upk_blocks = upkv_blocks[..., :head_size].reshape(
        block_count, adapter_rank, kv_heads * head_size
    )
    upv_blocks = upkv_blocks[..., head_size:].reshape(
        block_count, adapter_rank, kv_heads * head_size
    )
    query_row_block = adapted(frozen_queries, low_blocks[:, :, 0], upq_blocks)
    key_row_block = adapted(frozen_keys, low_blocks[:, :, 1], upk_blocks)
    value_row_block = adapted(frozen_values, low_blocks[:, :, 2], upv_blocks)
    grad_query, key_gradient, value_gradient = attention_grads(
        query_row_block.reshape(row_count, query_heads, head_size),
        key_row_block.reshape(row_count, kv_heads, head_size),
        value_row_block.reshape(row_count, kv_heads, head_size),
        attention_output_gradient.reshape(row_count, query_heads, head_size),
        document_numbers,
    )
    gq_blocks = grad_query.reshape(block_count, block_rows, -1)
    gk_blocks = key_gradient.reshape(block_count, block_rows, -1)
    gv_blocks = value_gradient.reshape(block_count, block_rows, -1)
    gradient_portion = ADAPTER_SCALE * jnp.concatenate(
        [
            jnp.einsum("brc,bkc->brk", gq_blocks, upq_blocks, precision=PRECISION_HIGH),
            jnp.einsum("brc,bkc->brk", gk_blocks, upk_blocks, precision=PRECISION_HIGH),
            jnp.einsum("brc,bkc->brk", gv_blocks, upv_blocks, precision=PRECISION_HIGH),
        ],
        axis=-1,
    )
    lowrank_grad = lax.psum(gradient_portion.reshape(row_count, 3 * adapter_rank), "mp")
    lowrank_gradient = lowrank_grad.reshape(block_count, block_rows, 3 * adapter_rank)
    down_terms = jnp.einsum("bri,brj->bij", row_blocks, lowrank_gradient, precision=PRECISION_HIGH)
    query_up_terms = ADAPTER_SCALE * jnp.einsum(
        "brk,brc->bkc", low_blocks[:, :, 0], gq_blocks, precision=PRECISION_HIGH
    )
    key_up_terms = ADAPTER_SCALE * jnp.einsum(
        "brk,brc->bkc", low_blocks[:, :, 1], gk_blocks, precision=PRECISION_HIGH
    )
    value_up_terms = ADAPTER_SCALE * jnp.einsum(
        "brk,brc->bkc", low_blocks[:, :, 2], gv_blocks, precision=PRECISION_HIGH
    )
    upkv_terms = jnp.concatenate(
        [
            key_up_terms.reshape(block_count, adapter_rank, kv_heads, head_size),
            value_up_terms.reshape(block_count, adapter_rank, kv_heads, head_size),
        ],
        axis=-1,
    )
    all_slots = lax.all_gather(block_tenant_slot, "dp", axis=0, tiled=True)
    senders = jnp.arange(dp_count * block_count, dtype=jnp.int32) // block_count
    owners = shard_tenant_table[senders, all_slots]
    down_in, upq_in, upkv_in = (
        lax.all_to_all(down_terms, "dp", split_axis=1, concat_axis=0, tiled=True),
        lax.all_to_all(query_up_terms, "dp", split_axis=1, concat_axis=0, tiled=True),
        lax.all_to_all(upkv_terms, "dp", split_axis=1, concat_axis=0, tiled=True),
    )
    owner_hot = (jnp.arange(count_of_tenants, dtype=jnp.int32)[:, None] == owners[None, :]).astype(
        jnp.float32
    )
    grad_down = jnp.einsum("tj,jrc->trc", owner_hot, down_in, precision=PRECISION_HIGH)
    grad_upq = jnp.einsum("tj,jrc->trc", owner_hot, upq_in, precision=PRECISION_HIGH)
    grad_upkv = jnp.einsum("tj,jrkc->trkc", owner_hot, upkv_in, precision=PRECISION_HIGH)
    return (grad_down, grad_upq, grad_upkv)


def solution(mesh):
    placed = (
        P("dp", "mp"),
        P("dp", "mp"),
        P("dp", "mp"),
        P("dp", "mp"),
        P("dp", "mp"),
        P(None, ("mp", "dp"), None),
        P(None, "dp", "mp"),
        P(None, "dp", "mp", None),
        P("dp"),
        P("dp"),
        P(),
    )
    return jax.shard_map(
        on_device,
        mesh=mesh,
        in_specs=placed,
        out_specs=(P(None, ("mp", "dp"), None), P(None, "dp", "mp"), P(None, "dp", "mp", None)),
        check_vma=False,
    )
```

profile of v0, /device:TPU:68, one launch (start us, length us, event | category | flops | bytes accessed | tf_op | source)
XLA Modules:
  0.0 654.9 jit_solution(5255772222505822899)
XLA Ops:
  7.2 0.9 copy.143
  8.2 0.8 copy.218
  9.1 0.8 gather_fusion.3
  9.8 0.8 copy.147
  10.6 17.7 %all-to-all-start.1 = ((f32[128,1,1,256]{3,2,1,0:T(1,128)}), f32[128,1,1,256]{3,2,1,0:T(1,128)S(1)}, u32[]{:S(2)}, u32[]{:S(2)}) async-start(f32[128,1,1,256]{3,2,1,0:T(1,128)} %copy.147), calls=%async_computation.1 | async-start | bytes 262144 | tf_op jit(solution)/shard_map/all_to_all | solution.py:79
  28.3 2.1 gather_fusion.1
  30.5 12.2 %all-to-all-done.1 = f32[128,1,1,256]{3,2,1,0:T(1,128)S(1)} async-done(((f32[128,1,1,256]{3,2,1,0:T(1,128)}), f32[128,1,1,256]{3,2,1,0:T(1,128)S(1)}, u32[]{:S(2)}, u32[]{:S(2)}) %all-to-all-start.1) | async-done | bytes 131104 | tf_op jit(solution)/shard_map/all_to_all | solution.py:79
  42.7 8.8 %all-to-all-start = ((f32[128,16,192]{2,1,0:T(8,128)}), f32[128,16,192]{2,1,0:T(8,128)S(1)}, u32[]{:S(2)}, u32[]{:S(2)}) async-start(f32[128,16,192]{2,1,0:T(8,128)} %gather_fusion.1), calls=%async_computation | async-start | bytes 4194304 | tf_op jit(solution)/shard_map/all_to_all | solution.py:73
  51.6 0.8 gather_fusion.5
  52.4 1.3 copy.149
  53.7 93.1 %all-to-all-done = f32[128,16,192]{2,1,0:T(8,128)S(1)} async-done(((f32[128,16,192]{2,1,0:T(8,128)}), f32[128,16,192]{2,1,0:T(8,128)S(1)}, u32[]{:S(2)}, u32[]{:S(2)}) %all-to-all-start) | async-done | bytes 1572896 | tf_op jit(solution)/shard_map/all_to_all | solution.py:73
  146.8 11.3 %all-to-all-start.2 = ((f32[128,1,1024]{2,1,0:T(1,128)}), f32[128,1,1024]{2,1,0:T(1,128)}, u32[]{:S(2)}, u32[]{:S(2)}) async-start(f32[128,1,1024]{2,1,0:T(1,128)} %copy.149), calls=%async_computation.2 | async-start | bytes 1048576 | tf_op jit(solution)/shard_map/all_to_all | solution.py:76
  158.4 1.5 copy.144
  159.9 2.0 copy.145
  161.9 2.1 gather_fusion.2
  164.1 2.9 fusion.45
  167.0 0.7 copy.146
  167.9 0.6 gather_fusion.4
  168.5 19.0 %all-to-all-done.2 = f32[128,1,1024]{2,1,0:T(1,128)} async-done(((f32[128,1,1024]{2,1,0:T(1,128)}), f32[128,1,1024]{2,1,0:T(1,128)}, u32[]{:S(2)}, u32[]{:S(2)}) %all-to-all-start.2) | async-done | bytes 524320 | tf_op jit(solution)/shard_map/all_to_all | solution.py:76
  187.5 1.2 copy.213
  188.7 0.6 gather_fusion.6
  189.3 69.0 %all-reduce.4.cloned.1.call-done = f32[3,128,3,64]{1,3,0,2:T(8,128)} async-done(((f32[3,128,3,64]{1,3,0,2:T(8,128)}), f32[3,128,3,64]{1,3,0,2:T(8,128)}) %all-reduce.4.cloned.1.call-update) | async-done | bytes 294928 | tf_op jit(solution)/shard_map/psum | solution.py:88
  258.3 1.4 convolution_multiply_fusion.3
  259.7 2.3 convolution_multiply_fusion
  262.1 0.3 fusion.14
  262.4 0.9 fusion.6
  263.3 1.0 fusion.5
  264.3 1.4 convolution_multiply_fusion.2
  265.8 2.0 fusion.10
  267.7 1.6 fusion
  269.4 1.6 fusion.9
  271.0 2.9 copy.157
  274.1 2.3 convolution_bitcast_fusion.3
  276.5 1.2 fusion.16
  277.7 1.3 fusion.15
  279.0 0.9 copy.168
  279.9 15.7 %all-to-all-start.5 = ((f32[3,64,1,256]{3,2,0,1:T(1,128)}), f32[3,64,1,256]{3,2,0,1:T(1,128)}, u32[]{:S(2)}, u32[]{:S(2)}) async-start(f32[3,64,1,256]{3,2,0,1:T(1,128)} %copy.168), calls=%async_computation.5 | async-start | bytes 393216 | tf_op jit(solution)/shard_map/all_to_all | solution.py:147
  295.6 1.8 convolution_bitcast_fusion.1
  297.4 3.0 copy.155
  300.4 1.6 reshape_reshape.11
  302.0 1.9 convolution_multiply_fusion.1
  303.9 1.5 copy.167
  305.4 6.7 %all-to-all-done.5 = f32[3,64,1,256]{3,2,0,1:T(1,128)} async-done(((f32[3,64,1,256]{3,2,0,1:T(1,128)}), f32[3,64,1,256]{3,2,0,1:T(1,128)}, u32[]{:S(2)}, u32[]{:S(2)}) %all-to-all-start.5) | async-done | bytes 196640 | tf_op jit(solution)/shard_map/all_to_all | solution.py:147
  312.1 9.5 %all-to-all-start.4 = ((f32[3,64,1024]{2,0,1:T(4,128)}), f32[3,64,1024]{2,0,1:T(4,128)}, u32[]{:S(2)}, u32[]{:S(2)}) async-start(f32[3,64,1024]{2,0,1:T(4,128)} %copy.167), calls=%async_computation.4 | async-start | bytes 2097152 | tf_op jit(solution)/shard_map/all_to_all | solution.py:146
  321.6 1.8 convolution_bitcast_fusion.6
  323.5 0.5 convolution_bitcast_fusion.5
  324.0 0.5 convolution_bitcast_fusion.4
  324.5 0.7 copy_bitcast_fusion.1
  325.2 89.0 %all-reduce.6.cloned.1.call-done = f32[3,128,192]{1,2,0:T(8,128)} async-done(((f32[3,128,192]{1,2,0:T(8,128)}), f32[3,128,192]{1,2,0:T(8,128)}) %all-reduce.6.cloned.1.call-update) | async-done | bytes 294928 | tf_op jit(solution)/shard_map/psum | solution.py:122
  414.3 2.3 convolution_bitcast_fusion
  416.6 3.2 copy.163
  419.8 15.8 %all-to-all-start.3 = ((f32[3,1024,192]{2,0,1:T(4,128)}), f32[3,1024,192]{2,0,1:T(4,128)}, u32[]{:S(2)}, u32[]{:S(2)}) async-start(f32[3,1024,192]{2,0,1:T(4,128)} %copy.163), calls=%async_computation.3 | async-start | bytes 8388608 | tf_op jit(solution)/shard_map/all_to_all | solution.py:145
  435.7 1.3 dynamic-slice
  437.8 195.0 %all-reduce = s32[192]{0:T(256)S(1)} all-reduce(s32[192]{0:T(256)S(1)} %dynamic-update-slice), channel_id=1, replica_groups=mesh['dp'=64,'mp'=8] {'dp'}, use_global_device_ids=true, to_apply=%add | all-reduce | flops 192 | bytes 1536
  632.9 2.2 gather_fusion
  635.1 0.9 copy.215
  636.5 0.7 copy.173
  637.2 1.6 reshape.190
  638.8 0.4 convolution_bitcast_fusion.2
  639.2 1.0 copy.172
  640.2 2.8 copy.164
  643.0 0.3 copy.165
  643.3 3.1 fusion.7
  646.5 1.6 copy.171
  (60 shorter events, 1.8 us)
Async XLA Ops:
  7.2 21.2 %copy-start = (f32[64,16,192]{2,1,0:T(8,128)S(1)}, f32[64,16,192]{2,1,0:T(8,128)}, u32[]{:S(2)}) copy-start(f32[64,16,192]{2,1,0:T(8,128)} %param.16) | copy-start | bytes 2359300
  10.6 32.1 %all-to-all-start.1 = ((f32[128,1,1,256]{3,2,1,0:T(1,128)}), f32[128,1,1,256]{3,2,1,0:T(1,128)S(1)}, u32[]{:S(2)}, u32[]{:S(2)}) async-start(f32[128,1,1,256]{3,2,1,0:T(1,128)} %copy.147), calls=%async_computation.1 | async-start | bytes 262144 | tf_op jit(solution)/shard_map/all_to_all | solution.py:79
  28.3 23.2 %copy-start.10 = (f32[64,1,1024]{2,1,0:T(1,128)S(1)}, f32[64,1,1024]{2,1,0:T(1,128)}, u32[]{:S(2)}) copy-start(f32[64,1,1024]{2,1,0:T(1,128)} %param.17) | copy-start | bytes 786436
  42.7 104.1 %all-to-all-start = ((f32[128,16,192]{2,1,0:T(8,128)}), f32[128,16,192]{2,1,0:T(8,128)S(1)}, u32[]{:S(2)}, u32[]{:S(2)}) async-start(f32[128,16,192]{2,1,0:T(8,128)} %gather_fusion.1), calls=%async_computation | async-start | bytes 4194304 | tf_op jit(solution)/shard_map/all_to_all | solution.py:73
  51.5 106.9 %copy-start.15 = (s32[3]{0:T(128)S(1)}, s32[3]{0:T(128)}, u32[]{:S(2)}) copy-start(s32[3]{0:T(128)} %param.20) | copy-start | bytes 40
  146.8 40.7 %all-to-all-start.2 = ((f32[128,1,1024]{2,1,0:T(1,128)}), f32[128,1,1024]{2,1,0:T(1,128)}, u32[]{:S(2)}, u32[]{:S(2)}) async-start(f32[128,1,1024]{2,1,0:T(1,128)} %copy.149), calls=%async_computation.2 | async-start | bytes 1048576 | tf_op jit(solution)/shard_map/all_to_all | solution.py:76
  158.1 100.2 %all-reduce.4.cloned.1.call-start = ((), (), s32[]{:S(2)}) async-start(), calls=%async_computation.6 | async-start | bytes 589824 | tf_op jit(solution)/shard_map/psum | solution.py:88
  159.9 4.1 copy-start.5
  161.9 5.8 copy-start.13
  164.1 95.6 %copy-start.11 = (bf16[384,128]{1,0:T(8,128)(2,1)S(1)}, bf16[384,128]{1,0:T(8,128)(2,1)}, u32[]{:S(2)}) copy-start(bf16[384,128]{1,0:T(8,128)(2,1)} %param.13) | copy-start | bytes 294916
  167.0 95.1 %copy-start.9 = (bf16[384,1024]{1,0:T(8,128)(2,1)S(1)}, bf16[384,1024]{1,0:T(8,128)(2,1)}, u32[]{:S(2)}) copy-start(bf16[384,1024]{1,0:T(8,128)(2,1)} %param.12) | copy-start | bytes 2359300
  168.5 95.8 %copy-start.6 = (f32[3,64,256]{2,1,0:T(8,128)}, f32[3,64,256]{2,1,0:T(8,128)S(1)}, u32[]{:S(2)}) copy-start(f32[3,64,256]{2,1,0:T(8,128)S(1)} %gather_fusion.4) | copy-start | bytes 589828
  189.3 70.4 %copy-start.3 = (f32[3,64,1024]{2,1,0:T(8,128)}, f32[3,64,1024]{2,1,0:T(8,128)S(1)}, u32[]{:S(2)}) copy-start(f32[3,64,1024]{2,1,0:T(8,128)S(1)} %gather_fusion.6) | copy-start | bytes 2359300
  262.4 3.3 copy-start.12
  263.3 2.4 copy-start.14
  279.9 32.2 %all-to-all-start.5 = ((f32[3,64,1,256]{3,2,0,1:T(1,128)}), f32[3,64,1,256]{3,2,0,1:T(1,128)}, u32[]{:S(2)}, u32[]{:S(2)}) async-start(f32[3,64,1,256]{3,2,0,1:T(1,128)} %copy.168), calls=%async_computation.5 | async-start | bytes 393216 | tf_op jit(solution)/shard_map/all_to_all | solution.py:147
  300.4 21.3 %copy-start.4 = (f32[3,64,1024]{2,1,0:T(8,128)S(1)}, f32[3,64,1024]{2,1,0:T(8,128)}, u32[]{:S(2)}) copy-start(f32[3,64,1024]{2,1,0:T(8,128)} %copy-done.3) | copy-start | bytes 2359300
  302.0 21.5 %copy-start.7 = (f32[3,64,256]{2,1,0:T(8,128)S(1)}, f32[3,64,256]{2,1,0:T(8,128)}, u32[]{:S(2)}) copy-start(f32[3,64,256]{2,1,0:T(8,128)} %copy-done.6) | copy-start | bytes 589828
  302.0 22.0 %copy-start.8 = (f32[384,128,1]{1,0,2:T(8,128)S(1)}, f32[384,128,1]{1,0,2:T(8,128)}, u32[]{:S(2)}) copy-start(f32[384,128,1]{1,0,2:T(8,128)} %fusion.10) | copy-start | bytes 589828
  312.1 107.7 %all-to-all-start.4 = ((f32[3,64,1024]{2,0,1:T(4,128)}), f32[3,64,1024]{2,0,1:T(4,128)}, u32[]{:S(2)}, u32[]{:S(2)}) async-start(f32[3,64,1024]{2,0,1:T(4,128)} %copy.167), calls=%async_computation.4 | async-start | bytes 2097152 | tf_op jit(solution)/shard_map/all_to_all | solution.py:146
  321.6 92.7 %all-reduce.6.cloned.1.call-start = ((), (), s32[]{:S(2)}) async-start(), calls=%async_computation.7 | async-start | bytes 589824 | tf_op jit(solution)/shard_map/psum | solution.py:122
  419.8 213.1 %copy-start.2 = (s32[64,2]{0,1:T(2,128)S(1)}, s32[64,2]{0,1:T(2,128)}, u32[]{:S(2)}) copy-start(s32[64,2]{0,1:T(2,128)} %param.21) | copy-start | bytes 1540
  419.8 220.4 %all-to-all-start.3 = ((f32[3,1024,192]{2,0,1:T(4,128)}), f32[3,1024,192]{2,0,1:T(4,128)}, u32[]{:S(2)}, u32[]{:S(2)}) async-start(f32[3,1024,192]{2,0,1:T(4,128)} %copy.163), calls=%async_computation.3 | async-start | bytes 8388608 | tf_op jit(solution)/shard_map/all_to_all | solution.py:145
  643.0 5.1 copy-start.1
Sparse Core Ops, SparseCore 0:
  167.9 90.3 all-reduce.3
  325.6 88.6 all-reduce.5
where the time goes:
time: 656 us; the launch traced here: 655 us
  waiting for transfers between devices  289 us (44%)
  blocking collectives  195 us (30%)
  starting transfers between devices  79.1 us (12%)
  local copies, waits for them, and re-layouts  42.8 us (7%)
  matrix products  29.8 us (5%)
  between operations  15.3 us (2%)
    unnamed x1, blocking collectives  195 us
    all_to_all x1, waiting for transfers between devices, on_device(): lax.all_to_all(adapter_down_weight[desired_result], 'dp', split_axis=0, c...  93.1 us
    psum x1, waiting for transfers between devices, on_device(): lax.psum(gradient_portion.reshape(row_count, 3 * adapter_rank), 'mp')  89 us
    psum x1, waiting for transfers between devices, on_device(): lowrank = lax.psum(partial_down.reshape(row_count, 3 * adapter_rank), 'mp')  69 us
    all_to_all x1, waiting for transfers between devices, on_device(): lax.all_to_all(adapter_up_query[desired_result], 'dp', split_axis=0, conc...  19 us
    all_to_all x1, starting transfers between devices, on_device(): lax.all_to_all(adapter_up_key_value[desired_result], 'dp', split_axis=0,...  17.7 us
    all_to_all x1, starting transfers between devices, on_device(): lax.all_to_all(down_terms, 'dp', split_axis=1, concat_axis=0, tiled=True)  15.8 us
    all_to_all x1, starting transfers between devices, on_device(): lax.all_to_all(upkv_terms, 'dp', split_axis=1, concat_axis=0, tiled=True)  15.7 us
  transfers between devices with their start and end apart: 8, of which 6 were waited for; matrix products, arithmetic and copies ran while one was open for 7% of the time, Pallas kernels for 0%

commit v1 on v0

--- a/solution.py
+++ b/solution.py
@@ -119,7 +119,9 @@
         ],
         axis=-1,
     )
-    lowrank_grad = lax.psum(gradient_portion.reshape(row_count, 3 * adapter_rank), "mp")
+    own = gradient_portion.reshape(row_count, 3 * adapter_rank)
+    shards = lax.all_gather(own, "mp", axis=0, tiled=False)
+    lowrank_grad = shards.sum(axis=0)
     lowrank_gradient = lowrank_grad.reshape(block_count, block_rows, 3 * adapter_rank)
     down_terms = jnp.einsum("bri,brj->bij", row_blocks, lowrank_gradient, precision=PRECISION_HIGH)
     query_up_terms = ADAPTER_SCALE * jnp.einsum(

time: 656 us -> 608 us (0.927)
  waiting for transfers between devices: 289 us -> 251 us
    psum x1 -> x0, waiting for transfers between devices: 89 us -> none  [on_device(): lax.psum(gradient_portion.reshape(row_count, 3 * adapter_rank), 'mp')]
    all_to_all x1, waiting for transfers between devices: 0.01 us -> 37.8 us  [on_device(): lax.all_to_all(query_up_terms, 'dp', split_axis=1, concat_axis=0, tiled=T...]
    all_to_all x1, waiting for transfers between devices: 6.69 us -> 14.1 us  [on_device(): lax.all_to_all(upkv_terms, 'dp', split_axis=1, concat_axis=0, tiled=True)]
  transfers between devices with their start and end apart: 8 -> 8, of which waited for: 6 -> 7; matrix products, arithmetic and copies ran while one was open for 7% -> 6% of each run, Pallas kernels for 0% -> 0%
where the time goes in v1:
time: 608 us; the launch traced here: 607 us
  waiting for transfers between devices  251 us (41%)
  blocking collectives  195 us (32%)
  starting transfers between devices  73.4 us (12%)
  local copies, waits for them, and re-layouts  41.3 us (7%)
  matrix products  25.1 us (4%)
  between operations  15.3 us (3%)
  other arithmetic  6.37 us (1%)
    unnamed x1, blocking collectives  195 us
    all_to_all x1, waiting for transfers between devices, on_device(): lax.all_to_all(adapter_down_weight[desired_result], 'dp', split_axis=0, c...  93.1 us
    psum x1, waiting for transfers between devices, on_device(): lowrank = lax.psum(partial_down.reshape(row_count, 3 * adapter_rank), 'mp')  68.7 us
    all_to_all x1, waiting for transfers between devices, on_device(): lax.all_to_all(query_up_terms, 'dp', split_axis=1, concat_axis=0, tiled=T...  37.8 us
    all_to_all x1, waiting for transfers between devices, on_device(): lax.all_to_all(adapter_up_query[desired_result], 'dp', split_axis=0, conc...  19 us
    all_to_all x1, starting transfers between devices, on_device(): lax.all_to_all(adapter_up_key_value[desired_result], 'dp', split_axis=0,...  17.7 us
    all_to_all x1, starting transfers between devices, on_device(): lax.all_to_all(upkv_terms, 'dp', split_axis=1, concat_axis=0, tiled=True)  15.5 us
    all_to_all x1, waiting for transfers between devices, on_device(): lax.all_to_all(upkv_terms, 'dp', split_axis=1, concat_axis=0, tiled=True)  14.1 us
  transfers between devices with their start and end apart: 8, of which 7 were waited for; matrix products, arithmetic and copies ran while one was open for 6% of the time, Pallas kernels for 0%

profile of v1, /device:TPU:68, one launch (start us, length us, event | category | flops | bytes accessed | tf_op | source)
XLA Modules:
  0.0 607.1 jit_solution(10726870892923768372)
XLA Ops:
  7.2 0.9 copy.143
  8.2 0.8 copy.214
  9.1 0.8 gather_fusion.3
  9.8 0.8 copy.147
  10.6 17.7 %all-to-all-start.1 = ((f32[128,1,1,256]{3,2,1,0:T(1,128)}), f32[128,1,1,256]{3,2,1,0:T(1,128)S(1)}, u32[]{:S(2)}, u32[]{:S(2)}) async-start(f32[128,1,1,256]{3,2,1,0:T(1,128)} %copy.147), calls=%async_computation.1 | async-start | bytes 262144 | tf_op jit(solution)/shard_map/all_to_all | solution.py:79
  28.3 2.1 gather_fusion.1
  30.4 12.3 %all-to-all-done.1 = f32[128,1,1,256]{3,2,1,0:T(1,128)S(1)} async-done(((f32[128,1,1,256]{3,2,1,0:T(1,128)}), f32[128,1,1,256]{3,2,1,0:T(1,128)S(1)}, u32[]{:S(2)}, u32[]{:S(2)}) %all-to-all-start.1) | async-done | bytes 131104 | tf_op jit(solution)/shard_map/all_to_all | solution.py:79
  42.7 8.8 %all-to-all-start = ((f32[128,16,192]{2,1,0:T(8,128)}), f32[128,16,192]{2,1,0:T(8,128)S(1)}, u32[]{:S(2)}, u32[]{:S(2)}) async-start(f32[128,16,192]{2,1,0:T(8,128)} %gather_fusion.1), calls=%async_computation | async-start | bytes 4194304 | tf_op jit(solution)/shard_map/all_to_all | solution.py:73
  51.6 0.8 gather_fusion.5
  52.4 1.3 copy.149
  53.7 93.1 %all-to-all-done = f32[128,16,192]{2,1,0:T(8,128)S(1)} async-done(((f32[128,16,192]{2,1,0:T(8,128)}), f32[128,16,192]{2,1,0:T(8,128)S(1)}, u32[]{:S(2)}, u32[]{:S(2)}) %all-to-all-start) | async-done | bytes 1572896 | tf_op jit(solution)/shard_map/all_to_all | solution.py:73
  146.8 11.3 %all-to-all-start.2 = ((f32[128,1,1024]{2,1,0:T(1,128)}), f32[128,1,1024]{2,1,0:T(1,128)}, u32[]{:S(2)}, u32[]{:S(2)}) async-start(f32[128,1,1024]{2,1,0:T(1,128)} %copy.149), calls=%async_computation.2 | async-start | bytes 1048576 | tf_op jit(solution)/shard_map/all_to_all | solution.py:76
  158.2 1.5 copy.144
  159.8 1.9 copy.145
  161.7 2.1 gather_fusion.2
  163.8 2.9 fusion.48
  166.7 0.7 copy.146
  167.9 0.6 gather_fusion.4
  168.5 19.0 %all-to-all-done.2 = f32[128,1,1024]{2,1,0:T(1,128)} async-done(((f32[128,1,1024]{2,1,0:T(1,128)}), f32[128,1,1024]{2,1,0:T(1,128)}, u32[]{:S(2)}, u32[]{:S(2)}) %all-to-all-start.2) | async-done | bytes 524320 | tf_op jit(solution)/shard_map/all_to_all | solution.py:76
  187.5 1.2 copy.210
  188.7 0.6 gather_fusion.6
  189.3 68.7 %all-reduce.3.cloned.1.call-done = f32[3,128,3,64]{1,3,0,2:T(8,128)} async-done(((f32[3,128,3,64]{1,3,0,2:T(8,128)}), f32[3,128,3,64]{1,3,0,2:T(8,128)}) %all-reduce.3.cloned.1.call-update) | async-done | bytes 294928 | tf_op jit(solution)/shard_map/psum | solution.py:88
  258.0 1.4 convolution_multiply_fusion.3
  259.5 2.3 convolution_multiply_fusion
  262.1 0.9 fusion.6
  263.1 1.0 fusion.5
  264.0 1.4 convolution_multiply_fusion.2
  265.5 2.0 fusion.10
  267.5 1.7 fusion
  269.2 1.6 fusion.9
  270.8 3.2 copy.157
  273.9 1.7 convolution_bitcast_fusion.1
  275.9 0.6 convolution_bitcast_fusion.3
  276.6 0.5 copy-done.6
  277.1 1.6 copy.155
  278.8 1.6 reshape_reshape.11
  280.4 1.8 fusion.49
  282.3 0.5 fusion.33
  283.0 0.5 fusion.34
  283.6 0.7 maximum_multiply_fusion
  284.4 0.3 fusion.16
  285.0 0.9 copy.168
  285.9 15.5 %all-to-all-start.5 = ((f32[3,64,1,256]{3,2,0,1:T(1,128)}), f32[3,64,1,256]{3,2,0,1:T(1,128)S(1)}, u32[]{:S(2)}, u32[]{:S(2)}) async-start(f32[3,64,1,256]{3,2,0,1:T(1,128)} %copy.168), calls=%async_computation.5 | async-start | bytes 393216 | tf_op jit(solution)/shard_map/all_to_all | solution.py:149
  301.4 1.0 convolution_multiply_fusion.1
  302.4 1.5 copy.167
  303.9 14.1 %all-to-all-done.5 = f32[3,64,1,256]{3,2,0,1:T(1,128)S(1)} async-done(((f32[3,64,1,256]{3,2,0,1:T(1,128)}), f32[3,64,1,256]{3,2,0,1:T(1,128)S(1)}, u32[]{:S(2)}, u32[]{:S(2)}) %all-to-all-start.5) | async-done | bytes 196640 | tf_op jit(solution)/shard_map/all_to_all | solution.py:149
  318.0 9.4 %all-to-all-start.4 = ((f32[3,64,1024]{2,0,1:T(4,128)}), f32[3,64,1024]{2,0,1:T(4,128)}, u32[]{:S(2)}, u32[]{:S(2)}) async-start(f32[3,64,1024]{2,0,1:T(4,128)} %copy.167), calls=%async_computation.4 | async-start | bytes 2097152 | tf_op jit(solution)/shard_map/all_to_all | solution.py:148
  327.5 5.6 all-gather.2.cloned.1.call-done
  333.1 2.5 reduce_sum.29
  335.6 2.0 convolution_bitcast_fusion
  337.7 3.2 copy.163
  340.9 37.8 %all-to-all-done.4 = f32[3,64,1024]{2,0,1:T(4,128)} async-done(((f32[3,64,1024]{2,0,1:T(4,128)}), f32[3,64,1024]{2,0,1:T(4,128)}, u32[]{:S(2)}, u32[]{:S(2)}) %all-to-all-start.4) | async-done | bytes 786464 | tf_op jit(solution)/shard_map/all_to_all | solution.py:148
  378.6 10.4 %all-to-all-start.3 = ((f32[3,1024,192]{2,0,1:T(4,128)}), f32[3,1024,192]{2,0,1:T(4,128)}, u32[]{:S(2)}, u32[]{:S(2)}) async-start(f32[3,1024,192]{2,0,1:T(4,128)} %copy.163), calls=%async_computation.3 | async-start | bytes 8388608 | tf_op jit(solution)/shard_map/all_to_all | solution.py:147
  389.1 1.3 dynamic-slice
  391.2 195.0 %all-reduce = s32[192]{0:T(256)S(1)} all-reduce(s32[192]{0:T(256)S(1)} %dynamic-update-slice), channel_id=1, replica_groups=mesh['dp'=64,'mp'=8] {'dp'}, use_global_device_ids=true, to_apply=%add | all-reduce | flops 192 | bytes 1536
  586.3 2.0 gather_fusion
  588.7 0.7 copy.173
  589.4 1.6 reshape.228
  591.0 0.4 convolution_bitcast_fusion.2
  591.4 1.0 copy.172
  592.4 2.8 copy.164
  595.2 0.3 copy.165
  595.5 3.1 fusion.7
  598.7 1.6 copy.171
  (73 shorter events, 2.8 us)
Async XLA Ops:
  7.2 21.2 %copy-start = (f32[64,16,192]{2,1,0:T(8,128)S(1)}, f32[64,16,192]{2,1,0:T(8,128)}, u32[]{:S(2)}) copy-start(f32[64,16,192]{2,1,0:T(8,128)} %param.16) | copy-start | bytes 2359300
  10.6 32.1 %all-to-all-start.1 = ((f32[128,1,1,256]{3,2,1,0:T(1,128)}), f32[128,1,1,256]{3,2,1,0:T(1,128)S(1)}, u32[]{:S(2)}, u32[]{:S(2)}) async-start(f32[128,1,1,256]{3,2,1,0:T(1,128)} %copy.147), calls=%async_computation.1 | async-start | bytes 262144 | tf_op jit(solution)/shard_map/all_to_all | solution.py:79
  30.4 21.1 %copy-start.14 = (f32[64,1,1024]{2,1,0:T(1,128)S(1)}, f32[64,1,1024]{2,1,0:T(1,128)}, u32[]{:S(2)}) copy-start(f32[64,1,1024]{2,1,0:T(1,128)} %param.17) | copy-start | bytes 786436
  42.7 104.1 %all-to-all-start = ((f32[128,16,192]{2,1,0:T(8,128)}), f32[128,16,192]{2,1,0:T(8,128)S(1)}, u32[]{:S(2)}, u32[]{:S(2)}) async-start(f32[128,16,192]{2,1,0:T(8,128)} %gather_fusion.1), calls=%async_computation | async-start | bytes 4194304 | tf_op jit(solution)/shard_map/all_to_all | solution.py:73
  51.6 106.6 %copy-start.19 = (s32[3]{0:T(128)S(1)}, s32[3]{0:T(128)}, u32[]{:S(2)}) copy-start(s32[3]{0:T(128)} %param.20) | copy-start | bytes 40
  146.8 40.7 %all-to-all-start.2 = ((f32[128,1,1024]{2,1,0:T(1,128)}), f32[128,1,1024]{2,1,0:T(1,128)}, u32[]{:S(2)}, u32[]{:S(2)}) async-start(f32[128,1,1024]{2,1,0:T(1,128)} %copy.149), calls=%async_computation.2 | async-start | bytes 1048576 | tf_op jit(solution)/shard_map/all_to_all | solution.py:76
  158.1 99.9 %all-reduce.3.cloned.1.call-start = ((), (), s32[]{:S(2)}) async-start(), calls=%async_computation.6 | async-start | bytes 589824 | tf_op jit(solution)/shard_map/psum | solution.py:88
  161.6 2.2 copy-start.7
  163.8 3.9 copy-start.17
  166.7 92.7 %copy-start.15 = (bf16[384,128]{1,0:T(8,128)(2,1)S(1)}, bf16[384,128]{1,0:T(8,128)(2,1)}, u32[]{:S(2)}) copy-start(bf16[384,128]{1,0:T(8,128)(2,1)} %param.13) | copy-start | bytes 294916
  167.5 165.6 %all-gather.2.cloned.1.call-start = ((), (), s32[]{:S(2)}) async-start(), calls=%async_computation.7 | async-start | bytes 2654208 | tf_op jit(solution)/shard_map/all_gather | solution.py:123
  167.9 93.9 %copy-start.13 = (bf16[384,1024]{1,0:T(8,128)(2,1)S(1)}, bf16[384,1024]{1,0:T(8,128)(2,1)}, u32[]{:S(2)}) copy-start(bf16[384,1024]{1,0:T(8,128)(2,1)} %param.12) | copy-start | bytes 2359300
  168.5 95.6 %copy-start.9 = (f32[3,64,256]{2,1,0:T(8,128)}, f32[3,64,256]{2,1,0:T(8,128)S(1)}, u32[]{:S(2)}) copy-start(f32[3,64,256]{2,1,0:T(8,128)S(1)} %gather_fusion.4) | copy-start | bytes 589828
  189.3 70.2 %copy-start.4 = (f32[3,64,1024]{2,1,0:T(8,128)}, f32[3,64,1024]{2,1,0:T(8,128)S(1)}, u32[]{:S(2)}) copy-start(f32[3,64,1024]{2,1,0:T(8,128)S(1)} %gather_fusion.6) | copy-start | bytes 2359300
  263.0 2.4 copy-start.16
  263.0 2.4 copy-start.18
  273.9 1.9 copy-start.3
  275.7 1.4 copy-start.6
  277.1 3.2 copy-start.5
  278.8 3.5 copy-start.10
  278.8 4.2 copy-start.12
  280.4 4.0 copy-start.11
  285.9 32.1 %all-to-all-start.5 = ((f32[3,64,1,256]{3,2,0,1:T(1,128)}), f32[3,64,1,256]{3,2,0,1:T(1,128)S(1)}, u32[]{:S(2)}, u32[]{:S(2)}) async-start(f32[3,64,1,256]{3,2,0,1:T(1,128)} %copy.168), calls=%async_computation.5 | async-start | bytes 393216 | tf_op jit(solution)/shard_map/all_to_all | solution.py:149
  303.9 31.7 %copy-start.8 = (bf16[384,1024]{1,0:T(8,128)(2,1)S(1)}, bf16[384,1024]{1,0:T(8,128)(2,1)}, u32[]{:S(2)}) copy-start(bf16[384,1024]{1,0:T(8,128)(2,1)} %param.11) | copy-start | bytes 2359300
  318.0 60.6 %all-to-all-start.4 = ((f32[3,64,1024]{2,0,1:T(4,128)}), f32[3,64,1024]{2,0,1:T(4,128)}, u32[]{:S(2)}, u32[]{:S(2)}) async-start(f32[3,64,1024]{2,0,1:T(4,128)} %copy.167), calls=%async_computation.4 | async-start | bytes 2097152 | tf_op jit(solution)/shard_map/all_to_all | solution.py:148
  340.9 245.4 %copy-start.2 = (s32[64,2]{0,1:T(2,128)S(1)}, s32[64,2]{0,1:T(2,128)}, u32[]{:S(2)}) copy-start(s32[64,2]{0,1:T(2,128)} %param.21) | copy-start | bytes 1540
  378.6 213.8 %all-to-all-start.3 = ((f32[3,1024,192]{2,0,1:T(4,128)}), f32[3,1024,192]{2,0,1:T(4,128)}, u32[]{:S(2)}, u32[]{:S(2)}) async-start(f32[3,1024,192]{2,0,1:T(4,128)} %copy.163), calls=%async_computation.3 | async-start | bytes 8388608 | tf_op jit(solution)/shard_map/all_to_all | solution.py:147
  595.5 4.8 copy-start.1
Sparse Core Ops, SparseCore 0:
  167.6 90.3 all-reduce.2
  284.5 48.5 all-gather.1
